TPU v7x, 32 devices: a whole 2x2x4 slice. The times are simulated.
32 devices in a mesh: group: 2 (over y), seq: 4 (over z), blk: 2 (over x), tp: 2 (over core).
Axes of the slice: x: 2, y: 2, z: 4, core: 2. Of those that a mesh axis runs over, the one named last changes fastest.
Arguments:
- tokens: bfloat16 [2048, 3072], P(('group', 'blk'), ('seq', 'tp')), parts along dimension 0, may hold values from -64 to 64
- timestep: int32 [2], P('group'), parts along dimension 0, may hold values from 25 to 49
- padded_heads: int32 [2], P('group'), parts along dimension 0, may hold values from 1 to 3
- modulation: float32 [50, 3, 3072], replicated, may hold values from -3 to 3
- qkv_weight: bfloat16 [3, 3072, 1024], P(None, 'blk', ('seq', 'tp')), may hold values from -1 to 1
- out_weight: bfloat16 [1024, 3072], P(('seq', 'tp'), 'blk'), may hold values from -0.5 to 0.5
Outputs:
- update: bfloat16 [2048, 3072], P(('group', 'blk'), ('seq', 'tp')), parts along dimension 0
There are 2 independent parts, one for each index of `group`. A program takes and returns all parts, laid end to end along the dimension named above; an argument that names none is the same for every part. Nothing has to cross between parts.
All inputs are finite; a program needn't handle non-finite values.
Results may differ from a plain program's by a relative error of at most 0.023.
Values may be sent and summed in bfloat16 or wider, within the bound.
A program may use at most 64 MiB of HBM per device.

v0:
```python
import math
import jax
import jax.numpy as jnp
from jax import lax
from jax.sharding import PartitionSpec as P

epsilon = 1e-06
neg_large = -1e30


def collect(own_part):
    gathered = lax.all_gather(own_part, ("seq", "tp"), axis=1, tiled=True)
    return gathered


def attend_block(running, queries, key_block, value_block, factor):
    largest, totals, weighted = running
    scores = (
        lax.dot_general(
            queries, key_block, (((1,), (1,)), ((), ())), preferred_element_type=jnp.float32
        )
        * factor
    )
    new_max = jnp.maximum(largest, jnp.max(scores, axis=1))
    rescale = jnp.exp(largest - new_max)
    weights = jnp.exp(scores - new_max[:, None])
    totals = totals * rescale + jnp.sum(weights, axis=1)
    weighted = weighted * rescale[:, None] + jnp.dot(
        weights.astype(jnp.bfloat16), value_block, preferred_element_type=jnp.float32
    )
    return (new_max, totals, weighted)


def body(tokens, timestep, padded_heads, modulation, qkv_weight, out_weight):
    slices = lax.axis_size(("seq", "tp"))
    own_index = lax.axis_index(("seq", "tp"))
    model_width = modulation.shape[2]
    own_width = model_width // slices
    token_rows = tokens.shape[0]
    head_size = out_weight.shape[0]
    table_row = lax.dynamic_index_in_dim(modulation, timestep[0], 0, keepdims=False)
    own_entry = lax.dynamic_slice_in_dim(table_row, own_index * own_width, own_width, 1)
    gathered = collect(tokens).astype(jnp.float32)
    average = jnp.mean(gathered, axis=1, keepdims=True)
    centered = gathered - average
    spread = jnp.mean(centered * centered, axis=1, keepdims=True)
    normed = centered * lax.rsqrt(spread + epsilon)
    modulated = (normed * (1.0 + table_row[1]) + table_row[0]).astype(jnp.bfloat16)
    projected = jnp.einsum(
        "td,kde->kte",
        modulated,
        lax.all_gather(qkv_weight, "blk", axis=1, tiled=True),
        preferred_element_type=jnp.float32,
    ).astype(jnp.bfloat16)
    queries = projected[0]
    factor = 1.0 / math.sqrt(head_size)
    initial = (
        jnp.full((token_rows,), neg_large, jnp.float32),
        jnp.zeros((token_rows,), jnp.float32),
        jnp.zeros((token_rows, head_size), jnp.float32),
    )
    key_piece = lax.all_gather(projected[1], "blk", axis=0, tiled=True)
    value_piece = lax.all_gather(projected[2], "blk", axis=0, tiled=True)
    length = key_piece.shape[0]

    def one_block(counter, inner_state):
        key_block = lax.dynamic_slice_in_dim(key_piece, counter * 512, 512, 0)
        value_block = lax.dynamic_slice_in_dim(value_piece, counter * 512, 512, 0)
        return attend_block(inner_state, queries, key_block, value_block, factor)

    largest, exp_totals, weighted = lax.fori_loop(0, length // 512, one_block, initial)
    attended = weighted / exp_totals[:, None]
    live_heads = slices - padded_heads[0]
    masked = jnp.where(own_index < live_heads, attended, 0.0).astype(jnp.bfloat16)
    head_term = jnp.dot(
        masked,
        lax.all_gather(out_weight, "blk", axis=1, tiled=True),
        preferred_element_type=jnp.float32,
    )
    summed = lax.psum_scatter(
        head_term.astype(jnp.bfloat16), ("seq", "tp"), scatter_dimension=1, tiled=True
    ).astype(jnp.float32)
    return (own_entry[2] * summed).astype(jnp.bfloat16)


def solution(mesh):
    return jax.shard_map(
        body,
        mesh=mesh,
        in_specs=(
            P(("group", "blk"), ("seq", "tp")),
            P("group"),
            P("group"),
            P(),
            P(None, "blk", ("seq", "tp")),
            P(("seq", "tp"), "blk"),
        ),
        out_specs=P(("group", "blk"), ("seq", "tp")),
        check_vma=False,
    )
```

profile of v0, /device:TPU:0, one launch (start us, length us, event | category | flops | bytes accessed | tf_op | source)
XLA Modules:
  0.0 157.3 jit_solution(16973399973763437814)
XLA Ops:
  6.5 0.0 all-gather.5.cloned.1.call-start
  6.5 0.7 all-gather.5.cloned.1.call-update
  7.3 0.0 all-gather.7.cloned.1.call-start
  7.3 0.7 all-gather.7.cloned.1.call-update
  8.0 0.0 reduce-scatter.4.cloned.1.call-start
  9.4 14.8 %all_gather.19 = bf16[128,3072]{1,0:T(8,128)(2,1)} all-gather(bf16[128,1536]{1,0:T(8,128)(2,1)} %param.13), channel_id=1, replica_groups=mesh['group'=2,'seq'=4,'blk'=2,'tp'=2] {'blk'}, dimensions={1}, use_global_device_ids=true | all-gather | bytes 1179648 | tf_op jit(solution)/shard_map/all_gather | solution.py:77
  24.1 1.0 dynamic-slice_add_fusion
  25.1 24.4 %all-gather.5.cloned.1.call-done = bf16[512,3072]{1,0:T(8,128)(2,1)} async-done(((bf16[512,384]{1,0:T(8,128)(2,1)}), bf16[512,3072]{1,0:T(8,128)(2,1)}) %all-gather.5.cloned.1.call-update) | async-done | bytes 3145744 | tf_op jit(solution)/shard_map/all_gather | solution.py:12
  49.5 0.0 copy-start
  49.5 2.5 %convert_reduce_fusion = f32[512]{0:T(512)S(1)} fusion(bf16[512,3072]{1,0:T(8,128)(2,1)} %all-gather.5.cloned.1.call-done), kind=kLoop, calls=%fused_computation.16 | loop fusion | flops 3145216 | bytes 3147776 | tf_op jit(solution)/shard_map/reduce_sum | solution.py:44
  52.0 0.3 copy-done
  52.3 1.0 fusion.11
  53.3 33.1 %all-gather.7.cloned.1.call-done = bf16[3,3072,128]{2,1,0:T(8,128)(2,1)} async-done(((bf16[3,1536,128]{2,1,0:T(8,128)(2,1)}), bf16[3,3072,128]{2,1,0:T(8,128)(2,1)}) %all-gather.7.cloned.1.call-update) | async-done | bytes 2359312 | tf_op jit(solution)/shard_map/all_gather | solution.py:52
  86.4 3.5 %fusion.21 = bf16[3,512,128]{2,1,0:T(8,128)(2,1)S(1)} fusion(bf16[3,3072,128]{2,1,0:T(8,128)(2,1)} %all-gather.7.cloned.1.call-done, bf16[512,3072]{1,0:T(8,128)(2,1)S(1)} %copy-done, f32[3072]{0:T(1024)S(1)} %bitcast.32, f32[3072]{0:T(1024)S(1)} %bitcast.31, f32[512]{0:T(512)S(1)} %add_rsqrt_fusion, f32[512]{0:T(512)S(1)} %broadcast_multiply_fusion), kind=kOutput, calls=%fused_computation.27 | convolution fusion | flops 1217593344 | bytes 5926912 | tf_op jit(solution)/shard_map/td,kde->kte/dot_general | solution.py:49
  90.0 5.7 %all-gather = bf16[1,1024,128]{2,1,0:T(8,128)(2,1)S(1)} all-gather(bf16[1,512,128]{2,1,0:T(8,128)(2,1)S(1)} %get-tuple-element.178), channel_id=2, replica_groups=mesh['group'=2,'seq'=4,'blk'=2,'tp'=2] {'blk'}, dimensions={1}, use_global_device_ids=true | all-gather | bytes 393216 | tf_op jit(solution)/shard_map/all_gather | solution.py:62
  95.7 5.6 %all-gather.1 = bf16[1,1024,128]{2,1,0:T(8,128)(2,1)S(1)} all-gather(bf16[1,512,128]{2,1,0:T(8,128)(2,1)S(1)} %get-tuple-element.176), channel_id=3, replica_groups=mesh['group'=2,'seq'=4,'blk'=2,'tp'=2] {'blk'}, dimensions={1}, use_global_device_ids=true | all-gather | bytes 393216 | tf_op jit(solution)/shard_map/all_gather | solution.py:63
  101.3 1.9 %while.18 = (s32[]{:T(128)}, f32[512]{0:T(512)S(1)}, f32[512]{0:T(512)S(1)}, f32[512,128]{1,0:T(8,128)S(1)}, bf16[1024,128]{1,0:T(8,128)(2,1)S(1)}, /*index=5*/b...) while((s32[]{:T(128)}, f32[512]{0:T(512)S(1)}, ...), condition=%wide.region_5.6_spmd.clone, body=%wide.region_2.5_spmd.clone.sunk | while | flops 135989760 | bytes 4096175 | solution.py:71
  101.3 0.3 fusion.42
  101.7 0.2 fusion.43
  101.9 0.4 convolution_add_fusion.2
  102.3 0.3 fusion.42
  102.6 0.2 fusion.43
  102.8 0.4 convolution_add_fusion.2
  103.2 2.2 %convolution_convert_fusion = bf16[512,3072]{1,0:T(8,128)(2,1)S(1)} fusion(bf16[128,3072]{1,0:T(8,128)(2,1)} %all_gather.19, f32[512,128]{1,0:T(8,128)S(1)} %get-tuple-element.130, f32[512]{0:T(512)S(1)} %get-tuple-element.131, pred[]{:T(512)S(6)} %lt.25), kind=kOutput, calls=%fused_computation.23 | convolution fusion | flops 404422656 | bytes 4196353 | tf_op jit(solution)/shard_map/dot_general | solution.py:75
  105.4 2.8 %copy.7 = bf16[512,3072]{0,1:T(8,128)(2,1)} copy(bf16[512,3072]{1,0:T(8,128)(2,1)S(1)} %convolution_convert_fusion) | data formatting | bytes 6291456
  108.2 0.0 reduce-scatter.4.cloned.1.call-update
  108.3 0.8 dynamic-slice_reduce_fusion
  109.1 39.7 %reduce-scatter.4.cloned.1.call-done = bf16[384,512]{1,0:T(8,128)(2,1)} async-done(((bf16[3072,512]{1,0:T(8,128)(2,1)}), bf16[384,512]{1,0:T(8,128)(2,1)}) %reduce-scatter.4.cloned.1.call-update) | async-done | bytes 393232
  148.8 1.2 copy.8
  150.0 0.8 multiply_convert_fusion
  (12 shorter events, 0.1 us)
Async XLA Ops:
  6.5 42.9 %all-gather.5.cloned.1.call-start = ((), (), s32[]{:S(2)}) async-start(), calls=%async_computation.1 | async-start | bytes 3538944 | tf_op jit(solution)/shard_map/all_gather | solution.py:12
  7.3 79.2 %all-gather.7.cloned.1.call-start = ((), (), s32[]{:S(2)}) async-start(), calls=%async_computation.2 | async-start | bytes 3538944 | tf_op jit(solution)/shard_map/all_gather | solution.py:52
  8.0 140.8 %reduce-scatter.4.cloned.1.call-start = ((), (), s32[]{:S(2)}) async-start(), calls=%async_computation.3 | async-start | bytes 3538944
  49.5 2.8 %copy-start = (bf16[512,3072]{1,0:T(8,128)(2,1)S(1)}, bf16[512,3072]{1,0:T(8,128)(2,1)}, u32[]{:S(2)}) copy-start(bf16[512,3072]{1,0:T(8,128)(2,1)} %all-gather.5.cloned.1.call-done) | copy-start | bytes 9437188
Sparse Core Ops, SparseCore 0:
  8.9 40.4 all-gather.4
  51.0 35.3 all-gather.6
  108.4 40.3 reduce-scatter.3
where the time goes:
time: 158 us; the launch traced here: 157 us
  waiting for transfers between devices  98.6 us (62%)
  blocking collectives  26.1 us (17%)
  between operations  14.5 us (9%)
  matrix products  7.03 us (4%)
  other arithmetic  5.73 us (4%)
  local copies, waits for them, and re-layouts  5.18 us (3%)
    unnamed x4, waiting for transfers between devices  41.1 us
    all_gather x1, waiting for transfers between devices, body(): lax.all_gather(qkv_weight, 'blk', axis=1, tiled=True)  33.1 us
    all_gather x1, waiting for transfers between devices, collect(): gathered = lax.all_gather(own_part, ('seq', 'tp'), axis=1, tiled=True)  24.4 us
    all_gather x1, blocking collectives, body(): lax.all_gather(out_weight, 'blk', axis=1, tiled=True)  14.8 us
    all_gather x1, blocking collectives, body(): key_piece = lax.all_gather(projected[1], 'blk', axis=0, tiled=True)  5.73 us
    all_gather x1, blocking collectives, body(): value_piece = lax.all_gather(projected[2], 'blk', axis=0, tiled=True)  5.62 us
    unnamed x4, local copies, waits for them, and re-layouts  4.33 us
    dot_general x1, matrix products, body(): jnp.einsum('td,kde->kte', modulated, lax.all_gather(qkv_weight, 'blk', ax...  3.52 us
  transfers between devices with their start and end apart: 3, of which 3 were waited for; matrix products, arithmetic and copies ran while one was open for 3% of the time, Pallas kernels for 0%

commit v1 on v0

--- a/solution.py
+++ b/solution.py
@@ -46,11 +46,29 @@
     spread = jnp.mean(centered * centered, axis=1, keepdims=True)
     normed = centered * lax.rsqrt(spread + epsilon)
     modulated = (normed * (1.0 + table_row[1]) + table_row[0]).astype(jnp.bfloat16)
-    projected = jnp.einsum(
-        "td,kde->kte",
-        modulated,
-        lax.all_gather(qkv_weight, "blk", axis=1, tiled=True),
-        preferred_element_type=jnp.float32,
+
+    def works_feed(my_data, mesh_dim, own_rows):
+        t1 = jax.lax.axis_index(mesh_dim)
+        piece_next = jax.lax.axis_size(mesh_dim)
+        d_next, carry, state_now = (piece_next, t1, my_data.shape[1])
+        x_now, u_next = (my_data, None)
+        grid = [(i, (i + 1) % d_next) for i in range(d_next)]
+        for b in range(d_next):
+            current_arr = jax.lax.ppermute(x_now, mesh_dim, grid) if b < d_next - 1 else None
+            lower = own_rows(x_now, (carry - b) % d_next * state_now)
+            u_next = lower if u_next is None else u_next + lower
+            x_now = current_arr
+        return u_next
+
+    projected = works_feed(
+        qkv_weight,
+        "blk",
+        lambda part, at: jnp.einsum(
+            "td,kde->kte",
+            lax.dynamic_slice_in_dim(modulated, at, part.shape[1], axis=1),
+            part,
+            preferred_element_type=jnp.float32,
+        ),
     ).astype(jnp.bfloat16)
     queries = projected[0]
     factor = 1.0 / math.sqrt(head_size)

time: 158 us -> 125 us (0.79)
  waiting for transfers between devices: 98.6 us -> 43.2 us
  blocking collectives: 26.1 us -> 45.3 us
  starting transfers between devices: 0.08 us -> 3.07 us
  other arithmetic: 5.73 us -> 7.53 us
    all_gather x1 -> x0, waiting for transfers between devices: 33.1 us -> none  [body(): lax.all_gather(qkv_weight, 'blk', axis=1, tiled=True)]
    all_gather x1, waiting for transfers between devices: 24.4 us -> 3.46 us  [collect(): gathered = lax.all_gather(own_part, ('seq', 'tp'), axis=1, tiled=True)]
    all_gather x1, blocking collectives: 14.8 us -> 33.4 us  [body(): lax.all_gather(out_weight, 'blk', axis=1, tiled=True)]
    ppermute x0 -> x1, starting transfers between devices: none -> 3.03 us  [works_feed(): jax.lax.ppermute(x_now, mesh_dim, grid)]
    convert_element_type x0 -> x1, other arithmetic: none -> 1.81 us  [body(): (normed * (1.0 + table_row[1]) + table_row[0]).astype(jnp.bfloat16)]
    dot_general x1 -> x2, matrix products: 3.52 us -> 1.98 us  [body(): jnp.einsum('td,kde->kte', lax.dynamic_slice_in_dim(modulated, at, part.sh...]
    unnamed x4 -> x3, waiting for transfers between devices: 41.1 us -> 39.8 us
    unnamed x4 -> x6, local copies, waits for them, and re-layouts: 4.33 us -> 4.34 us
  transfers between devices with their start and end apart: 3 -> 3, of which waited for: 3 -> 2; matrix products, arithmetic and copies ran while one was open for 3% -> 6% of each run, Pallas kernels for 0% -> 0%
where the time goes in v1:
time: 125 us
  blocking collectives  45.3 us (36%)
  waiting for transfers between devices  43.2 us (35%)
  between operations  14.8 us (12%)
  other arithmetic  7.53 us (6%)
  matrix products  5.51 us (4%)
  local copies, waits for them, and re-layouts  5.19 us (4%)
  starting transfers between devices  3.07 us (2%)
    unnamed x3, waiting for transfers between devices  39.8 us
    all_gather x1, blocking collectives, body(): lax.all_gather(out_weight, 'blk', axis=1, tiled=True)  33.4 us
    all_gather x1, blocking collectives, body(): key_piece = lax.all_gather(projected[1], 'blk', axis=0, tiled=True)  6.29 us
    all_gather x1, blocking collectives, body(): value_piece = lax.all_gather(projected[2], 'blk', axis=0, tiled=True)  5.62 us
    unnamed x6, local copies, waits for them, and re-layouts  4.34 us
    all_gather x1, waiting for transfers between devices, collect(): gathered = lax.all_gather(own_part, ('seq', 'tp'), axis=1, tiled=True)  3.46 us
    ppermute x1, starting transfers between devices, works_feed(): jax.lax.ppermute(x_now, mesh_dim, grid)  3.03 us
    reduce_sum x1, other arithmetic, body(): average = jnp.mean(gathered, axis=1, keepdims=True)  2.53 us
  transfers between devices with their start and end apart: 3, of which 2 were waited for; matrix products, arithmetic and copies ran while one was open for 6% of the time, Pallas kernels for 0%

profile of v1, /device:TPU:0, one launch (start us, length us, event | category | flops | bytes accessed | tf_op | source)
XLA Modules:
  0.0 124.7 jit_solution(224733968441123272)
XLA Ops:
  6.5 0.0 all-gather.4.cloned.1.call-start
  6.5 0.7 all-gather.4.cloned.1.call-update
  7.3 0.0 reduce-scatter.4.cloned.1.call-start
  7.3 3.0 %collective-permute-start = (bf16[3,1536,128]{2,1,0:T(8,128)(2,1)}, bf16[3,1536,128]{2,1,0:T(8,128)(2,1)S(1)}, u32[]{:S(2)}, u32[]{:S(2)}) collective-permute-start(bf16[3,1536,128]{2,1,0:T(8,128)(2,1)} %param.12), channel_id=1, source_target_pairs={{0,2},{2,0},{1,3},{3,1},{4,6},{6,4},{5,7},{7,5},{8,10},{10,8},{9,1... | collective-permute-start | bytes 3538952 | tf_op jit(solution)/shard_map/ppermute | solution.py:57
  11.7 33.4 %all_gather.15 = bf16[128,3072]{1,0:T(8,128)(2,1)} all-gather(bf16[128,1536]{1,0:T(8,128)(2,1)} %param.13), channel_id=1, replica_groups=mesh['group'=2,'seq'=4,'blk'=2,'tp'=2] {'blk'}, dimensions={1}, use_global_device_ids=true | all-gather | bytes 1179648 | tf_op jit(solution)/shard_map/all_gather | solution.py:95
  45.0 1.0 dynamic-slice_add_fusion
  46.0 3.5 %all-gather.4.cloned.1.call-done = bf16[512,3072]{1,0:T(8,128)(2,1)} async-done(((bf16[512,384]{1,0:T(8,128)(2,1)}), bf16[512,3072]{1,0:T(8,128)(2,1)}) %all-gather.4.cloned.1.call-update) | async-done | bytes 3145744 | tf_op jit(solution)/shard_map/all_gather | solution.py:12
  49.5 0.0 copy-start
  49.5 2.5 %convert_reduce_fusion = f32[512]{0:T(512)S(1)} fusion(bf16[512,3072]{1,0:T(8,128)(2,1)} %all-gather.4.cloned.1.call-done), kind=kLoop, calls=%fused_computation.16 | loop fusion | flops 3145216 | bytes 3147776 | tf_op jit(solution)/shard_map/reduce_sum | solution.py:44
  52.0 0.3 copy-done
  52.3 1.0 fusion.11
  53.3 0.0 copy-start.1
  53.3 1.8 %fusion.14 = bf16[512,3072]{1,0:T(8,128)(2,1)S(1)} fusion(bf16[512,3072]{1,0:T(8,128)(2,1)S(1)} %copy-done, f32[3072]{0:T(1024)S(1)} %bitcast.38, f32[3072]{0:T(1024)S(1)} %bitcast.37, f32[512]{0:T(512)S(1)} %add_rsqrt_fusion, f32[512]{0:T(512)S(1)} %broadcast_multiply_fusion), kind=kLoop, calls=%fused_computation.22 | loop fusion | flops 9437184 | bytes 6320128 | tf_op jit(solution)/shard_map/convert_element_type | solution.py:48
  55.1 0.0 copy-done.1
  55.1 1.0 fusion.17
  56.1 0.0 collective-permute-done
  56.1 1.0 fusion.27
  57.1 6.3 %all-gather = bf16[1,1024,128]{2,1,0:T(8,128)(2,1)S(1)} all-gather(bf16[1,512,128]{2,1,0:T(8,128)(2,1)S(1)} %get-tuple-element.178), channel_id=2, replica_groups=mesh['group'=2,'seq'=4,'blk'=2,'tp'=2] {'blk'}, dimensions={1}, use_global_device_ids=true | all-gather | bytes 393216 | tf_op jit(solution)/shard_map/all_gather | solution.py:80
  63.4 5.6 %all-gather.1 = bf16[1,1024,128]{2,1,0:T(8,128)(2,1)S(1)} all-gather(bf16[1,512,128]{2,1,0:T(8,128)(2,1)S(1)} %get-tuple-element.176), channel_id=3, replica_groups=mesh['group'=2,'seq'=4,'blk'=2,'tp'=2] {'blk'}, dimensions={1}, use_global_device_ids=true | all-gather | bytes 393216 | tf_op jit(solution)/shard_map/all_gather | solution.py:81
  69.1 1.9 %while.18 = (s32[]{:T(128)}, f32[512]{0:T(512)S(1)}, f32[512]{0:T(512)S(1)}, f32[512,128]{1,0:T(8,128)S(1)}, bf16[1024,128]{1,0:T(8,128)(2,1)S(1)}, /*index=5*/b...) while((s32[]{:T(128)}, f32[512]{0:T(512)S(1)}, ...), condition=%wide.region_5.6_spmd.clone, body=%wide.region_2.5_spmd.clone.sunk | while | flops 135989760 | bytes 4096175 | solution.py:89
  69.1 0.3 fusion.51
  69.4 0.2 fusion.52
  69.6 0.4 convolution_add_fusion.2
  70.0 0.3 fusion.51
  70.3 0.2 fusion.52
  70.6 0.4 convolution_add_fusion.2
  71.0 2.2 %convolution_convert_fusion = bf16[512,3072]{1,0:T(8,128)(2,1)S(1)} fusion(bf16[128,3072]{1,0:T(8,128)(2,1)} %all_gather.15, f32[512,128]{1,0:T(8,128)S(1)} %get-tuple-element.130, f32[512]{0:T(512)S(1)} %get-tuple-element.131, pred[]{:T(512)S(6)} %lt.41), kind=kOutput, calls=%fused_computation.23 | convolution fusion | flops 404422656 | bytes 4196353 | tf_op jit(solution)/shard_map/dot_general | solution.py:93
  73.1 2.8 %copy.7 = bf16[512,3072]{0,1:T(8,128)(2,1)} copy(bf16[512,3072]{1,0:T(8,128)(2,1)S(1)} %convolution_convert_fusion) | data formatting | bytes 6291456
  76.0 0.0 reduce-scatter.4.cloned.1.call-update
  76.0 0.8 dynamic-slice_reduce_fusion
  76.8 39.0 %reduce-scatter.4.cloned.1.call-done = bf16[384,512]{1,0:T(8,128)(2,1)} async-done(((bf16[3072,512]{1,0:T(8,128)(2,1)}), bf16[384,512]{1,0:T(8,128)(2,1)}) %reduce-scatter.4.cloned.1.call-update) | async-done | bytes 393232
  115.8 1.2 copy.8
  117.1 0.8 multiply_convert_fusion
  (12 shorter events, 0.1 us)
Async XLA Ops:
  6.5 42.9 %all-gather.4.cloned.1.call-start = ((), (), s32[]{:S(2)}) async-start(), calls=%async_computation.1 | async-start | bytes 3538944 | tf_op jit(solution)/shard_map/all_gather | solution.py:12
  7.3 108.6 %reduce-scatter.4.cloned.1.call-start = ((), (), s32[]{:S(2)}) async-start(), calls=%async_computation.2 | async-start | bytes 3538944
  7.3 48.8 %collective-permute-start = (bf16[3,1536,128]{2,1,0:T(8,128)(2,1)}, bf16[3,1536,128]{2,1,0:T(8,128)(2,1)S(1)}, u32[]{:S(2)}, u32[]{:S(2)}) collective-permute-start(bf16[3,1536,128]{2,1,0:T(8,128)(2,1)} %param.12), channel_id=1, source_target_pairs={{0,2},{2,0},{1,3},{3,1},{4,6},{6,4},{5,7},{7,5},{8,10},{10,8},{9,1... | collective-permute-start | bytes 3538952 | tf_op jit(solution)/shard_map/ppermute | solution.py:57
  49.5 2.8 %copy-start = (bf16[512,3072]{1,0:T(8,128)(2,1)S(1)}, bf16[512,3072]{1,0:T(8,128)(2,1)}, u32[]{:S(2)}) copy-start(bf16[512,3072]{1,0:T(8,128)(2,1)} %all-gather.4.cloned.1.call-done) | copy-start | bytes 9437188
  53.3 1.8 %copy-start.1 = (bf16[3,1536,128]{2,1,0:T(8,128)(2,1)S(1)}, bf16[3,1536,128]{2,1,0:T(8,128)(2,1)}, u32[]{:S(2)}) copy-start(bf16[3,1536,128]{2,1,0:T(8,128)(2,1)} %param.12) | copy-start | bytes 3538948
Sparse Core Ops, SparseCore 0:
  8.9 40.4 all-gather.3
  76.1 39.6 reduce-scatter.3
